TPU v7x, 32 devices: a whole 2x2x4 slice. The times are simulated.
32 devices in a mesh: shard: 2 (over y), ctx: 4 (over z), tp: 4 (over x, core).
Axes of the slice: x: 2, y: 2, z: 4, core: 2. Of those that a mesh axis runs over, the one named last changes fastest.
Arguments:
- inputs: bfloat16 [2, 4096, 768], P('shard', 'ctx'), may hold values from -6 to 6
- lengths: int32 [2], P('shard'), may hold values from 1024 to 4096, as said below
- global_blocks: int32 [2, 2], P('shard'), may hold values from 0 to 15, as said below
- random_blocks: int32 [2, 64, 3], P('shard', 'ctx'), may hold values from 0 to 63
- master_blocks: float32 [768, 96, 96], P(('shard', 'ctx', 'tp'))
- outer_vectors: float32 [6, 768], replicated
- inner_biases: float32 [4, 1152], P('tp'), may hold values from -4 to 4
- left_stats: float32 [768, 96, 96], P(('shard', 'ctx', 'tp')), as said below
- right_stats: float32 [768, 96, 96], P(('shard', 'ctx', 'tp')), as said below
- left_roots: float32 [768, 96, 96], P(('shard', 'ctx', 'tp')), as said below
- right_roots: float32 [768, 96, 96], P(('shard', 'ctx', 'tp')), as said below
- cotangent: bfloat16 [2, 4096, 768], P('shard', 'ctx'), may hold values from -6 to 6
Outputs:
- output: bfloat16 [2, 4096, 768], P('shard', 'ctx')
- input_grad: bfloat16 [2, 4096, 768], P('shard', 'ctx')
- block_grads: float32 [768, 96, 96], P(('shard', 'ctx', 'tp'))
- outer_grads: float32 [6, 768], P(None, ('shard', 'ctx'))
- inner_grads: float32 [4, 1152], P('tp', ('shard', 'ctx'))
- maxima: float32 [12], P('tp')
- left_new: float32 [768, 96, 96], P(('shard', 'ctx', 'tp'))
- right_new: float32 [768, 96, 96], P(('shard', 'ctx', 'tp'))
- new_blocks: float32 [768, 96, 96], P(('shard', 'ctx', 'tp'))
- new_outer: float32 [6, 768], P(None, ('shard', 'ctx'))
- new_inner: float32 [4, 1152], P('tp', ('shard', 'ctx'))
Inputs may be any that keep to these rules, and one draw needn't show every extreme that they name: `lengths`: sequence 0 holds 4096 valid tokens. `global_blocks`: the two ids of a sequence differ. `left_stats`: each block is symmetric. `right_stats`: each block is symmetric. `left_roots`: each block is symmetric. `right_roots`: each block is symmetric.
All inputs are finite; a program needn't handle non-finite values.
Results may differ from a plain program's by a relative error of at most 0.018.
Values may be sent and summed in bfloat16 or wider, within the bound.
No kernel may reach another device: no remote copies, remote signals or barrier semaphores. Data moves between devices by JAX's collectives and lax.ppermute only.
A program may use at most 192 MiB of HBM per device.

v0:
```python
import jax
import jax.numpy as jnp
from jax import lax
from jax.sharding import PartitionSpec as P

D = 768
HEADS = 12
HEAD = 64
FF = 3072
BLOCK = 64
SEQ = 4096
PB = 96
eps_norm = 1e-06
tau_clip = 9.0
rate_matrix = 0.3
rate_vector = 0.001
neg_large = -1e30
high = lax.Precision.HIGHEST


def layer_norm(values, gain, shift):
    mean_val = jnp.mean(values, axis=-1, keepdims=True)
    centred = values - mean_val
    var_val = jnp.mean(centred * centred, axis=-1, keepdims=True)
    return centred * lax.rsqrt(var_val + eps_norm) * gain + shift


def gelu_tanh(values):
    return jax.nn.gelu(values, approximate=True)


def to_grid(blocks, row_count, col_count):
    shaped = blocks.reshape(row_count // PB, col_count // PB, PB, PB)
    return shaped.transpose(0, 2, 1, 3).reshape(row_count, col_count)


def from_grid(matrix):
    row_count, col_count = matrix.shape
    shaped = matrix.reshape(row_count // PB, PB, col_count // PB, PB)
    return shaped.transpose(0, 2, 1, 3).reshape(-1, PB, PB)


def unpack_weights(whole, head_cols, unit_count):
    first_end = D // PB * (3 * head_cols // PB)
    second_end = first_end + head_cols // PB * (D // PB)
    third_end = second_end + D // PB * (unit_count // PB)
    return (
        to_grid(whole[:first_end], D, 3 * head_cols),
        to_grid(whole[first_end:second_end], head_cols, D),
        to_grid(whole[second_end:third_end], D, unit_count),
        to_grid(whole[third_end:], unit_count, D),
    )


def block_layout(slot_length, global_ids, random_ids, first_block, rows_blocks, block_count):
    rows = first_block + jnp.arange(rows_blocks, dtype=jnp.int32)
    window = jnp.stack([rows - 1, rows, rows + 1], axis=1)
    globals_row = jnp.broadcast_to(global_ids[None, :], (rows_blocks, 2))
    listed = jnp.concatenate([window, globals_row, random_ids], axis=1)
    inside = (listed >= 0) & (listed < block_count)
    clipped = jnp.clip(listed, 0, block_count - 1)
    key_pos = listed[:, :, None] * BLOCK + jnp.arange(BLOCK, dtype=jnp.int32)[None, None, :]
    key_mask = (inside[:, :, None] & (key_pos < slot_length)).reshape(rows_blocks, -1)
    query_pos = (first_block * BLOCK + jnp.arange(rows_blocks * BLOCK, dtype=jnp.int32)).reshape(
        rows_blocks, BLOCK
    )
    return (clipped, key_mask, query_pos < slot_length)


def pick_blocks(full_rows, clipped, head_count):
    block_count = full_rows.shape[0] // BLOCK
    picked = full_rows.reshape(block_count, BLOCK, -1)[clipped]
    return picked.reshape(clipped.shape[0], clipped.shape[1] * BLOCK, head_count, HEAD)


def attend_scores(query_blocks, key_blocks):
    return jnp.einsum(
        "lqhd,lkhd->lhqk", query_blocks, key_blocks, preferred_element_type=jnp.float32
    ) * HEAD ** (-0.5)


def probs_again(query_blocks, d_out_blocks, key_blocks, value_blocks, key_mask, lse_blk):
    raw_scores = attend_scores(query_blocks, key_blocks)
    probs = jnp.exp(jnp.where(key_mask[:, None, None, :], raw_scores, neg_large) - lse_blk)
    d_probs = jnp.einsum(
        "lqhd,lkhd->lhqk", d_out_blocks, value_blocks, preferred_element_type=jnp.float32
    )
    return (probs, d_probs)


def group_back(
    query_blocks,
    d_out_blocks,
    key_src,
    value_src,
    clipped,
    key_mask,
    lse_blk,
    delta_blk,
    block_count,
):
    rows_blocks, _, heads_here, _ = query_blocks.shape
    head_cols = heads_here * HEAD
    key_blocks = pick_blocks(key_src, clipped, heads_here)
    value_blocks = pick_blocks(value_src, clipped, heads_here)
    probs, d_probs = probs_again(
        query_blocks, d_out_blocks, key_blocks, value_blocks, key_mask, lse_blk
    )
    delta_blk = jnp.sum(probs * d_probs, axis=-1, keepdims=True)
    d_scores = (probs * (d_probs - delta_blk)).astype(jnp.bfloat16)
    d_query = jnp.einsum(
        "lhqk,lkhd->lqhd", d_scores, key_blocks, preferred_element_type=jnp.float32
    ) * HEAD ** (-0.5)
    d_key_blocks = jnp.einsum(
        "lhqk,lqhd->lkhd", d_scores, query_blocks, preferred_element_type=jnp.float32
    ) * HEAD ** (-0.5)
    d_value_blocks = jnp.einsum(
        "lhqk,lqhd->lkhd",
        probs.astype(jnp.bfloat16),
        d_out_blocks,
        preferred_element_type=jnp.float32,
    )
    listed_count = clipped.shape[1]
    d_key_full = (
        jnp.zeros((block_count, BLOCK, head_cols), jnp.float32)
        .at[clipped]
        .add(d_key_blocks.reshape(rows_blocks, listed_count, BLOCK, head_cols))
    )
    d_value_full = (
        jnp.zeros((block_count, BLOCK, head_cols), jnp.float32)
        .at[clipped]
        .add(d_value_blocks.reshape(rows_blocks, listed_count, BLOCK, head_cols))
    )
    return (
        d_query.reshape(-1, head_cols),
        d_key_full.reshape(-1, head_cols),
        d_value_full.reshape(-1, head_cols),
    )


def per_device(
    inputs,
    lengths,
    global_blocks,
    random_blocks,
    master_blocks,
    outer_vectors,
    inner_biases,
    left_stats,
    right_stats,
    left_roots,
    right_roots,
    cotangent,
):
    tensor_count = lax.axis_size("tp")
    owner_count = lax.axis_size(("shard", "ctx"))
    heads_here = HEADS // tensor_count
    head_cols = heads_here * HEAD
    unit_count = FF // tensor_count
    slot_count, ctx_tokens, _ = inputs.shape
    rows_blocks = ctx_tokens // BLOCK
    block_count = SEQ // BLOCK
    ctx_index = lax.axis_index("ctx")
    owner_index = lax.axis_index(("shard", "ctx"))
    gathered = lax.all_gather(
        master_blocks.astype(jnp.bfloat16), ("shard", "ctx"), axis=0, tiled=True
    )
    w_qkv, w_out, w_up, w_down = unpack_weights(gathered, head_cols, unit_count)
    flat_in = inputs.reshape(-1, D)
    inner_row = inner_biases[0]
    q_bias = inner_row[:head_cols]
    v_bias = inner_row[head_cols : 2 * head_cols]
    up_bias = inner_row[2 * head_cols :]
    projected = jnp.dot(flat_in, w_qkv, preferred_element_type=jnp.float32)
    queries = (projected[:, :head_cols] + q_bias).astype(jnp.bfloat16)
    key_rows = (
        projected[:, head_cols : 2 * head_cols]
        .astype(jnp.bfloat16)
        .reshape(slot_count, ctx_tokens, head_cols)
    )
    value_rows = (
        (projected[:, 2 * head_cols :] + v_bias)
        .astype(jnp.bfloat16)
        .reshape(slot_count, ctx_tokens, head_cols)
    )
    keys_all, values_all = (
        lax.all_gather(key_rows, "ctx", axis=1, tiled=True),
        lax.all_gather(value_rows, "ctx", axis=1, tiled=True),
    )
    query_slots = queries.reshape(slot_count, ctx_tokens, head_cols)
    peak_logit = jnp.full((heads_here,), neg_large, jnp.float32)
    slot_index = 0
    clipped, key_mask, query_mask = block_layout(
        lengths[slot_index],
        global_blocks[slot_index],
        random_blocks[slot_index],
        ctx_index * rows_blocks,
        rows_blocks,
        block_count,
    )
    layouts = [(clipped, key_mask)]
    query_blocks = query_slots[slot_index].reshape(rows_blocks, BLOCK, heads_here, HEAD)
    key_blocks = pick_blocks(keys_all[slot_index], clipped, heads_here)
    value_blocks = pick_blocks(values_all[slot_index], clipped, heads_here)
    raw_scores = attend_scores(query_blocks, key_blocks)
    both_mask = key_mask[:, None, None, :] & query_mask[:, None, :, None]
    peak_logit = jnp.maximum(
        peak_logit, jnp.max(jnp.where(both_mask, raw_scores, neg_large), axis=(0, 2, 3))
    )
    masked = jnp.where(key_mask[:, None, None, :], raw_scores, neg_large)
    row_top = jnp.max(masked, axis=-1, keepdims=True)
    shifted = jnp.exp(masked - row_top)
    row_total = jnp.sum(shifted, axis=-1, keepdims=True)
    probs = shifted / row_total
    lse_list = [row_top + jnp.log(row_total)]
    attended = jnp.einsum(
        "lhqk,lkhd->lqhd",
        probs.astype(jnp.bfloat16),
        value_blocks,
        preferred_element_type=jnp.float32,
    )
    attended_list = attended.reshape(ctx_tokens, head_cols)
    attended_low = attended_list.astype(jnp.bfloat16)
    branch = (
        lax.psum(jnp.dot(attended_low, w_out, preferred_element_type=jnp.float32), "tp")
        + outer_vectors[0]
    )
    hidden_in = flat_in.astype(jnp.float32) + branch
    x_first = layer_norm(hidden_in, outer_vectors[2], outer_vectors[3])
    x_first_low = x_first.astype(jnp.bfloat16)
    gate_pre = jnp.dot(x_first_low, w_up, preferred_element_type=jnp.float32) + up_bias
    act_low = gelu_tanh(gate_pre).astype(jnp.bfloat16)
    ff_out = (
        lax.psum(jnp.dot(act_low, w_down, preferred_element_type=jnp.float32), "tp")
        + outer_vectors[1]
    )
    mixed_sum = x_first + ff_out
    result = layer_norm(mixed_sum, outer_vectors[4], outer_vectors[5])
    maxima = lax.pmax(peak_logit, ("shard", "ctx"))
    positions = ctx_index * ctx_tokens + jnp.arange(ctx_tokens, dtype=jnp.int32)
    row_valid = (positions[None, :] < lengths[:, None]).astype(jnp.float32).reshape(-1)
    d_result = cotangent.reshape(-1, D).astype(jnp.float32) * row_valid[:, None]
    regathered = lax.all_gather(
        master_blocks.astype(jnp.bfloat16), ("shard", "ctx"), axis=0, tiled=True
    )
    wb_qkv, wb_out, wb_up, wb_down = unpack_weights(regathered, head_cols, unit_count)
    _, back_second = jax.vjp(layer_norm, mixed_sum, outer_vectors[4], outer_vectors[5])
    d_mixed, d_gain2, d_shift2 = back_second(d_result)
    d_ff_low = d_mixed.astype(jnp.bfloat16)
    d_bias2 = jnp.sum(d_ff_low.astype(jnp.float32), axis=0)
    g_down = jnp.dot(act_low.T, d_ff_low, preferred_element_type=jnp.float32)
    d_act = jnp.dot(d_ff_low, wb_down.T, preferred_element_type=jnp.float32)
    _, back_gelu = jax.vjp(gelu_tanh, gate_pre)
    d_gate_low = back_gelu(d_act)[0].astype(jnp.bfloat16)
    d_upbias = jnp.sum(d_gate_low.astype(jnp.float32), axis=0)
    g_up = jnp.dot(x_first_low.T, d_gate_low, preferred_element_type=jnp.float32)
    d_first = d_mixed + lax.psum(
        jnp.dot(d_gate_low, wb_up.T, preferred_element_type=jnp.float32), "tp"
    )
    _, back_first = jax.vjp(layer_norm, hidden_in, outer_vectors[2], outer_vectors[3])
    d_hidden, d_gain1, d_shift1 = back_first(d_first)
    d_branch_low = d_hidden.astype(jnp.bfloat16)
    d_bias_out = jnp.sum(d_branch_low.astype(jnp.float32), axis=0)
    g_out = jnp.dot(attended_low.T, d_branch_low, preferred_element_type=jnp.float32)
    d_att_low = jnp.dot(d_branch_low, wb_out.T, preferred_element_type=jnp.float32).astype(
        jnp.bfloat16
    )
    d_att_slots = d_att_low.reshape(slot_count, ctx_tokens, head_cols)
    keys_back, values_back = (keys_all, values_all)
    slot_index = 0
    clipped, key_mask = layouts[slot_index]
    query_blocks = query_slots[slot_index].reshape(rows_blocks, BLOCK, heads_here, HEAD)
    d_out_blocks = d_att_slots[slot_index].reshape(rows_blocks, BLOCK, heads_here, HEAD)
    d_query, d_key_full, d_value_full = group_back(
        query_blocks,
        d_out_blocks,
        keys_back[slot_index],
        values_back[slot_index],
        clipped,
        key_mask,
        lse_list[slot_index],
        None,
        block_count,
    )
    dk_list = [d_key_full]
    dv_list = [d_value_full]
    d_keys, d_values = (
        lax.psum_scatter(
            jnp.stack(dk_list).astype(jnp.bfloat16), "ctx", scatter_dimension=1, tiled=True
        ).astype(jnp.float32),
        lax.psum_scatter(
            jnp.stack(dv_list).astype(jnp.bfloat16), "ctx", scatter_dimension=1, tiled=True
        ).astype(jnp.float32),
    )
    d_q_low = d_query.astype(jnp.bfloat16)
    d_k_low = d_keys.reshape(-1, head_cols).astype(jnp.bfloat16)
    d_v_low = d_values.reshape(-1, head_cols).astype(jnp.bfloat16)
    d_proj = jnp.concatenate([d_q_low, d_k_low, d_v_low], axis=1)
    d_qbias = jnp.sum(d_q_low.astype(jnp.float32), axis=0)
    d_vbias = jnp.sum(d_v_low.astype(jnp.float32), axis=0)
    g_qkv = jnp.dot(flat_in.T, d_proj, preferred_element_type=jnp.float32)
    d_inputs = d_hidden + lax.psum(
        jnp.dot(d_proj, wb_qkv.T, preferred_element_type=jnp.float32).astype(jnp.bfloat16), "tp"
    ).astype(jnp.float32)
    input_grad = d_inputs.reshape(inputs.shape).astype(jnp.bfloat16)
    blocks_grad = jnp.concatenate(
        [from_grid(g_qkv), from_grid(g_out), from_grid(g_up), from_grid(g_down)], axis=0
    )
    outer_part = jnp.stack([d_bias_out, d_bias2, d_gain1, d_shift1, d_gain2, d_shift2], axis=0)
    inner_part = jnp.concatenate([d_qbias, d_vbias, d_upbias])[None, :]
    block_sum, outer_sum, inner_sum = (
        lax.psum_scatter(blocks_grad, ("shard", "ctx"), scatter_dimension=0, tiled=True),
        lax.psum_scatter(outer_part, ("shard", "ctx"), scatter_dimension=1, tiled=True),
        lax.psum_scatter(inner_part, ("shard", "ctx"), scatter_dimension=1, tiled=True),
    )
    left_new = 0.5 * left_stats + 0.5 * jnp.einsum(
        "bij,bkj->bik", block_sum, block_sum, precision=high
    )
    right_new = 0.5 * right_stats + 0.5 * jnp.einsum(
        "bji,bjk->bik", block_sum, block_sum, precision=high
    )
    left_applied = jnp.einsum("bij,bjk->bik", left_roots, block_sum, precision=high)
    step_val = jnp.einsum("bij,bjk->bik", left_applied, right_roots, precision=high)
    clip_sqrt = jnp.sqrt(tau_clip / jnp.maximum(maxima, tau_clip))
    head_factor = jnp.repeat(clip_sqrt, HEAD)
    table = jnp.concatenate([head_factor, head_factor, jnp.ones((head_cols,), jnp.float32)])
    qkv_factor = jnp.tile(table.reshape(1, -1, PB), (D // PB, 1, 1)).reshape(-1, PB)
    blocks_here = master_blocks.shape[0]
    all_factor = jnp.concatenate(
        [qkv_factor, jnp.ones((blocks_here * owner_count - qkv_factor.shape[0], PB), jnp.float32)],
        axis=0,
    )
    own_factor = lax.dynamic_slice_in_dim(all_factor, owner_index * blocks_here, blocks_here, 0)
    new_blocks = (master_blocks - rate_matrix * step_val) * own_factor[:, None, :]
    outer_cols = D // owner_count
    own_outer = lax.dynamic_slice_in_dim(outer_vectors, owner_index * outer_cols, outer_cols, 1)
    new_outer = own_outer - rate_vector * outer_sum
    inner_cols = inner_biases.shape[1] // owner_count
    inner_factor = jnp.concatenate([head_factor, jnp.ones((head_cols + unit_count,), jnp.float32)])
    own_inner_factor = lax.dynamic_slice_in_dim(
        inner_factor, owner_index * inner_cols, inner_cols, 0
    )
    own_inner = lax.dynamic_slice_in_dim(inner_biases, owner_index * inner_cols, inner_cols, 1)
    new_inner = (own_inner - rate_vector * inner_sum) * own_inner_factor[None, :]
    output = result.reshape(inputs.shape).astype(jnp.bfloat16)
    return (
        output,
        input_grad,
        block_sum,
        outer_sum,
        inner_sum,
        maxima,
        left_new,
        right_new,
        new_blocks,
        new_outer,
        new_inner,
    )


def solution(mesh):
    return jax.shard_map(
        per_device,
        mesh=mesh,
        in_specs=(
            P("shard", "ctx", None),
            P("shard"),
            P("shard", None),
            P("shard", "ctx", None),
            P(("shard", "ctx", "tp"), None, None),
            P(),
            P("tp", None),
            P(("shard", "ctx", "tp"), None, None),
            P(("shard", "ctx", "tp"), None, None),
            P(("shard", "ctx", "tp"), None, None),
            P(("shard", "ctx", "tp"), None, None),
            P("shard", "ctx", None),
        ),
        out_specs=(
            P("shard", "ctx", None),
            P("shard", "ctx", None),
            P(("shard", "ctx", "tp"), None, None),
            P(None, ("shard", "ctx")),
            P("tp", ("shard", "ctx")),
            P("tp"),
            P(("shard", "ctx", "tp"), None, None),
            P(("shard", "ctx", "tp"), None, None),
            P(("shard", "ctx", "tp"), None, None),
            P(None, ("shard", "ctx")),
            P("tp", ("shard", "ctx")),
        ),
        check_vma=False,
    )
```

profile of v0, /device:TPU:0, one launch (start us, length us, event | category | flops | bytes accessed | tf_op | source)
XLA Modules:
  0.0 1027.7 jit_solution(3224889106006550222)
XLA Ops:
  9.6 83.2 %all-gather.6.cloned.1.call-done = bf16[192,96,96]{2,1,0:T(8,128)(2,1)} async-done(((bf16[24,96,96]{2,1,0:T(8,128)(2,1)}), bf16[192,96,96]{2,1,0:T(8,128)(2,1)}) %all-gather.6.cloned.1.call-update) | async-done | bytes 3538960 | tf_op jit(solution)/shard_map/all_gather | solution.py:165
  95.8 2.8 fusion.29
  109.1 27.4 %all-gather.10.cloned.1.call-done = bf16[4096,192]{0,1:T(8,128)(2,1)} async-done(((bf16[1024,192]{0,1:T(8,128)(2,1)}), bf16[4096,192]{0,1:T(8,128)(2,1)}) %all-gather.10.cloned.1.call-update) | async-done | bytes 1572880 | tf_op jit(solution)/shard_map/all_gather | solution.py:187
  136.5 3.1 copy.103
  142.4 15.9 %reshape.559 = bf16[16,512,3,64]{3,2,1,0:T(4,128)(2,1)} reshape(bf16[128,64,192]{2,1,0:T(8,128)(2,1)} %gather_fusion.1) | data formatting | bytes 6291456 | tf_op jit(solution)/shard_map/reshape | solution.py:73
  158.4 12.2 %copy.106 = bf16[16,512,3,64]{1,3,2,0:T(8,128)(2,1)} copy(bf16[16,512,3,64]{3,2,1,0:T(4,128)(2,1)} %reshape.559) | data formatting | bytes 6291456 | tf_op jit(solution)/shard_map/reshape | solution.py:73
  170.6 4.1 all-gather.8.cloned.1.call-done
  174.6 3.1 copy.98
  180.5 15.9 %reshape.558 = bf16[16,512,3,64]{3,2,1,0:T(4,128)(2,1)} reshape(bf16[128,64,192]{2,1,0:T(8,128)(2,1)} %gather_fusion) | data formatting | bytes 6291456 | tf_op jit(solution)/shard_map/reshape | solution.py:73
  196.4 12.3 %copy.107 = bf16[16,512,3,64]{1,3,2,0:T(8,128)(2,1)} copy(bf16[16,512,3,64]{3,2,1,0:T(4,128)(2,1)} %reshape.558) | data formatting | bytes 6291456 | tf_op jit(solution)/shard_map/reshape | solution.py:73
  208.7 3.2 fusion.24
  212.0 3.6 select_reduce_fusion
  227.7 3.8 reshape.488
  233.3 3.9 reshape.490
  237.2 52.6 %all-reduce.7.cloned.1.call-done = f32[1024,768]{1,0:T(8,128)} async-done(((f32[1024,768]{1,0:T(8,128)}), f32[1024,768]{1,0:T(8,128)}) %all-reduce.7.cloned.1.call-update) | async-done | bytes 3145744 | tf_op jit(solution)/shard_map/psum | solution.py:225
  297.7 3.8 fusion.59
  302.4 67.8 %all-reduce.9.cloned.1.call-done = f32[1024,768]{1,0:T(8,128)} async-done(((f32[1024,768]{1,0:T(8,128)}), f32[1024,768]{1,0:T(8,128)}) %all-reduce.9.cloned.1.call-update) | async-done | bytes 3145744 | tf_op jit(solution)/shard_map/psum | solution.py:234
  370.2 3.9 fusion.63
  377.8 2.8 fusion.62
  384.2 4.3 convert_reduce_fusion
  389.6 3.1 fusion.69
  393.6 67.9 %all-reduce.11.cloned.1.call-done = f32[1024,768]{1,0:T(8,128)} async-done(((f32[1024,768]{1,0:T(8,128)}), f32[1024,768]{1,0:T(8,128)}) %all-reduce.11.cloned.1.call-update) | async-done | bytes 3145744 | tf_op jit(solution)/shard_map/psum | solution.py:257
  461.5 5.4 multiply_reduce_fusion.1
  473.4 7.2 fusion.20
  480.6 15.1 %copy.136 = f32[16,512,3,64]{3,2,1,0:T(4,128)} copy(f32[16,512,3,64]{1,3,2,0:T(8,128)} %fusion.20) | data formatting | bytes 12582912 | tf_op jit(solution)/shard_map/reshape | solution.py:132
  495.7 18.9 %reshape.553 = f32[128,64,192]{2,1,0:T(8,128)} reshape(f32[16,512,3,64]{3,2,1,0:T(4,128)} %copy.136) | data formatting | bytes 12582912 | tf_op jit(solution)/shard_map/reshape | solution.py:132
  517.0 26.2 %scatter_fusion.1 = f32[64,64,192]{2,1,0:T(8,128)} fusion(f32[64,64,192]{2,1,0:T(8,128)} %broadcast.358.clone, s32[128]{0:T(128)S(1)} %reshape.508, f32[128,64,192]{2,1,0:T(8,128)} %reshape.553), kind=kCustom, calls=%fused_computation.3 | custom fusion | flops 1572864 | bytes 18874880 | tf_op jit(solution)/shard_map/scatter-add | solution.py:132
  548.7 6.7 multiply_reduce_fusion
  555.4 3.9 multiply_convert_fusion
  560.9 3.6 multiply_bitcast_fusion
  564.5 15.1 %copy.135 = f32[16,512,3,64]{3,2,1,0:T(4,128)} copy(f32[16,512,3,64]{1,3,2,0:T(8,128)} %multiply_bitcast_fusion) | data formatting | bytes 12582912 | tf_op jit(solution)/shard_map/reshape | solution.py:127
  579.6 18.9 %reshape.552 = f32[128,64,192]{2,1,0:T(8,128)} reshape(f32[16,512,3,64]{3,2,1,0:T(4,128)} %copy.135) | data formatting | bytes 12582912 | tf_op jit(solution)/shard_map/reshape | solution.py:127
  601.0 26.2 %scatter_fusion = f32[64,64,192]{2,1,0:T(8,128)} fusion(f32[64,64,192]{2,1,0:T(8,128)} %broadcast.358.clone.1, s32[128]{0:T(128)S(1)} %reshape.508, f32[128,64,192]{2,1,0:T(8,128)} %reshape.552), kind=kCustom, calls=%fused_computation.2 | custom fusion | flops 1572864 | bytes 18874880 | tf_op jit(solution)/shard_map/scatter-add | solution.py:127
  629.6 2.8 copy.119
  632.7 4.3 fusion.58
  639.5 4.3 copy.127
  647.8 4.3 copy.126
  664.6 3.4 reduce-scatter.10.cloned.1.call-done
  668.0 4.1 convolution_convert_fusion
  681.3 7.7 pad_maximum_fusion
  689.7 19.4 %pmax.7 = f32[3]{0:T(128)S(1)} all-reduce(f32[3]{0:T(128)S(1)} %broadcast_maximum_fusion), channel_id=1, replica_groups=mesh['shard'=2,'ctx'=4,'tp'=4] {'shard','ctx'}, use_global_device_ids=true, to_apply=%region_32.33 | all-reduce | flops 3 | bytes 24 | tf_op jit(solution)/shard_map/pmax | solution.py:239
  710.0 22.3 %reduce-scatter.16.cloned.1.call-done = f32[96,6]{1,0:T(8,128)} async-done(((f32[768,6]{1,0:T(8,128)}), f32[96,6]{1,0:T(8,128)}) %reduce-scatter.16.cloned.1.call-update) | async-done | bytes 2320
  734.6 63.3 %reduce-scatter.18.cloned.1.call-done = f32[144,1]{1,0:T(8,128)} async-done(((f32[1152,1]{1,0:T(8,128)}), f32[144,1]{1,0:T(8,128)}) %reduce-scatter.18.cloned.1.call-update) | async-done | bytes 592
  800.1 42.6 %all-reduce.13.cloned.1.call-done = bf16[1024,768]{1,0:T(8,128)(2,1)} async-done(((bf16[1024,768]{1,0:T(8,128)(2,1)}), bf16[1024,768]{1,0:T(8,128)(2,1)}) %all-reduce.13.cloned.1.call-update) | async-done | bytes 1572880 | tf_op jit(solution)/shard_map/psum | solution.py:302
  842.7 3.9 fusion.26
  846.7 162.3 %reduce-scatter.14.cloned.1.call-done = f32[24,96,96]{2,1,0:T(8,128)} async-done(((f32[192,96,96]{2,1,0:T(8,128)}), f32[24,96,96]{2,1,0:T(8,128)}) %reduce-scatter.14.cloned.1.call-update) | async-done | bytes 884752 | tf_op jit(solution)/shard_map/reduce_scatter | solution.py:312
  1013.9 3.2 fusion.36
  1017.0 3.6 fusion.37
  (301 shorter events, 112.5 us)
Async XLA Ops:
  7.2 1001.7 %copy-start = (f32[24,96,96]{2,1,0:T(8,128)S(1)}, f32[24,96,96]{2,1,0:T(8,128)}, u32[]{:S(2)}) copy-start(f32[24,96,96]{2,1,0:T(8,128)} %param.21) | copy-start | bytes 2654212
  7.2 85.6 %all-gather.6.cloned.1.call-start = ((), (), s32[]{:S(2)}) async-start(), calls=%async_computation.5 | async-start | bytes 5308416 | tf_op jit(solution)/shard_map/all_gather | solution.py:165
  9.5 127.0 %all-gather.10.cloned.1.call-start = ((), (), s32[]{:S(2)}) async-start(), calls=%async_computation.14 | async-start | bytes 1966080 | tf_op jit(solution)/shard_map/all_gather | solution.py:187
  95.8 5.2 copy-start.65
  95.8 5.2 copy-start.64
  100.9 6.9 slice-start.1
  101.0 73.7 %all-gather.8.cloned.1.call-start = ((), (), s32[]{:S(2)}) async-start(), calls=%async_computation.13 | async-start | bytes 1966080 | tf_op jit(solution)/shard_map/all_gather | solution.py:188
  103.4 186.4 %all-reduce.7.cloned.1.call-start = ((), (), s32[]{:S(2)}) async-start(), calls=%async_computation.6 | async-start | bytes 6291456 | tf_op jit(solution)/shard_map/psum | solution.py:225
  196.4 12.3 %copy-start.12 = (bf16[16,64,3,64]{1,0,3,2:T(8,128)(2,1)S(1)}, bf16[16,64,3,64]{1,0,3,2:T(8,128)(2,1)}, u32[]{:S(2)}) copy-start(bf16[16,64,3,64]{1,0,3,2:T(8,128)(2,1)} %reshape_squeeze_reshape.7) | copy-start | bytes 1179652
  212.0 4.2 copy-start.7
  222.3 147.8 %all-reduce.9.cloned.1.call-start = ((), (), s32[]{:S(2)}) async-start(), calls=%async_computation.7 | async-start | bytes 6291456 | tf_op jit(solution)/shard_map/psum | solution.py:234
  223.9 68.9 %copy-start.43 = (f32[768]{0:T(1024)}, f32[768]{0:T(1024)S(1)}, u32[]{:S(2)}) copy-start(f32[768]{0:T(1024)S(1)} %get-tuple-element.22) | copy-start | bytes 9220
  223.9 68.9 %copy-start.49 = (f32[768]{0:T(1024)}, f32[768]{0:T(1024)S(1)}, u32[]{:S(2)}) copy-start(f32[768]{0:T(1024)S(1)} %get-tuple-element.21) | copy-start | bytes 9220
  233.3 56.5 %copy-start.23 = (bf16[1,1024,768]{2,1,0:T(8,128)(2,1)S(1)}, bf16[1,1024,768]{2,1,0:T(8,128)(2,1)}, u32[]{:S(2)}) copy-start(bf16[1,1024,768]{2,1,0:T(8,128)(2,1)} %param.12) | copy-start | bytes 4718596
  301.5 160.0 %all-reduce.11.cloned.1.call-start = ((), (), s32[]{:S(2)}) async-start(), calls=%async_computation.8 | async-start | bytes 6291456 | tf_op jit(solution)/shard_map/psum | solution.py:257
  380.6 7.9 copy-start.5
  380.6 7.9 copy-start.45
  381.5 7.0 copy-start.26
  392.8 68.7 %copy-start.42 = (f32[1024]{0:T(1024)S(1)}, f32[1024]{0:T(1024)}, u32[]{:S(2)}) copy-start(f32[1024]{0:T(1024)} %copy-done.41) | copy-start | bytes 12292
  392.8 68.7 %copy-start.44 = (f32[768]{0:T(1024)S(1)}, f32[768]{0:T(1024)}, u32[]{:S(2)}) copy-start(f32[768]{0:T(1024)} %copy-done.43) | copy-start | bytes 9220
  392.8 68.7 %copy-start.46 = (f32[1024]{0:T(1024)S(1)}, f32[1024]{0:T(1024)}, u32[]{:S(2)}) copy-start(f32[1024]{0:T(1024)} %copy-done.45) | copy-start | bytes 12292
  392.8 269.5 %reduce-scatter.12.cloned.1.call-start = ((), (), s32[]{:S(2)}) async-start(), calls=%async_computation.10 | async-start | bytes 1966080 | tf_op jit(solution)/shard_map/reduce_scatter | solution.py:291
  393.6 73.3 %copy-start.51 = (f32[1024]{0:T(1024)S(1)}, f32[1024]{0:T(1024)}, u32[]{:S(2)}) copy-start(f32[1024]{0:T(1024)} %copy-done.50) | copy-start | bytes 12292
  461.5 5.4 copy-start.3
  473.4 7.2 copy-start.11
  548.4 119.6 %reduce-scatter.10.cloned.1.call-start = ((), (), s32[]{:S(2)}) async-start(), calls=%async_computation.9 | async-start | bytes 1966080 | tf_op jit(solution)/shard_map/reduce_scatter | solution.py:288
  555.4 5.5 copy-start.13
  632.4 99.9 %reduce-scatter.16.cloned.1.call-start = ((), (), s32[]{:S(2)}) async-start(), calls=%async_computation.15 | async-start | bytes 442368
  639.5 4.3 copy-start.25
  639.5 4.3 copy-start.78
  645.3 6.9 copy-start.56
  647.8 4.9 copy-start.60
  647.8 5.5 copy-start.59
  647.8 6.0 copy-start.9
  647.8 6.0 copy-start.10
  655.7 5.4 copy-start.57
  655.7 5.4 copy-start.54
  655.7 5.4 copy-start.53
  659.4 8.6 copy-start.36
  662.2 135.6 %reduce-scatter.18.cloned.1.call-start = ((), (), s32[]{:S(2)}) async-start(), calls=%async_computation.16 | async-start | bytes 663552
  664.6 178.1 %all-reduce.13.cloned.1.call-start = ((), (), s32[]{:S(2)}) async-start(), calls=%async_computation.11 | async-start | bytes 3145728 | tf_op jit(solution)/shard_map/psum | solution.py:302
  668.0 4.5 copy-start.17
  668.0 4.5 copy-start.20
  672.1 336.8 %reduce-scatter.14.cloned.1.call-start = ((), (), s32[]{:S(2)}) async-start(), calls=%async_computation.12 | async-start | bytes 10616832 | tf_op jit(solution)/shard_map/reduce_scatter | solution.py:312
  733.2 109.5 %copy-start.58 = (f32[6,96]{1,0:T(8,128)}, f32[6,96]{1,0:T(8,128)S(1)}, u32[]{:S(2)}) copy-start(f32[6,96]{1,0:T(8,128)S(1)} %copy.138) | copy-start | bytes 6916
  798.8 43.9 %copy-start.66 = (f32[1,144]{1,0:T(1,128)}, f32[1,144]{1,0:T(1,128)S(1)}, u32[]{:S(2)}) copy-start(f32[1,144]{1,0:T(1,128)S(1)} %copy.140) | copy-start | bytes 1732
  846.7 164.8 %copy-start.18 = (f32[24,96,96]{2,1,0:T(8,128)S(1)}, f32[24,96,96]{2,1,0:T(8,128)}, u32[]{:S(2)}) copy-start(f32[24,96,96]{2,1,0:T(8,128)} %param.16) | copy-start | bytes 2654212
  846.7 164.8 %copy-start.27 = (f32[24,96,96]{2,1,0:T(8,128)S(1)}, f32[24,96,96]{2,1,0:T(8,128)}, u32[]{:S(2)}) copy-start(f32[24,96,96]{2,1,0:T(8,128)} %param.22) | copy-start | bytes 2654212
  (45 other events, 98.8 us)
Sparse Core Ops, SparseCore 0:
  10.7 82.0 all-gather.5
  101.1 35.3 all-gather.9
  138.7 35.9 all-gather.7
  222.5 67.2 all-reduce.6
  301.6 68.5 all-reduce.8
  392.9 68.5 all-reduce.10
  548.5 35.4 reduce-scatter.11
  632.5 35.4 reduce-scatter.9
  671.3 61.0 reduce-scatter.15
  736.0 61.7 reduce-scatter.17
  800.8 41.8 all-reduce.12
  846.7 162.1 reduce-scatter.13
where the time goes:
time: 1030 us
  waiting for transfers between devices  597 us (58%)
  local copies, waits for them, and re-layouts  215 us (21%)
  other arithmetic  108 us (10%)
  matrix products  69.6 us (7%)
  blocking collectives  19.4 us (2%)
  between operations  16.1 us (2%)
    reduce_scatter x1, waiting for transfers between devices, per_device(): lax.psum_scatter(blocks_grad, ('shard', 'ctx'), scatter_dimension=0, tile...  162 us
    unnamed x14, waiting for transfers between devices  85.7 us
    all_gather x1, waiting for transfers between devices, per_device(): lax.all_gather(master_blocks.astype(jnp.bfloat16), ('shard', 'ctx'), axis...  83.2 us
    psum x1, waiting for transfers between devices, per_device(): lax.psum(jnp.dot(d_gate_low, wb_up.T, preferred_element_type=jnp.float32)...  67.9 us
    psum x1, waiting for transfers between devices, per_device(): lax.psum(jnp.dot(act_low, w_down, preferred_element_type=jnp.float32), 'tp')  67.8 us
    reshape x4, local copies, waits for them, and re-layouts, pick_blocks(): picked.reshape(clipped.shape[0], clipped.shape[1] * BLOCK, head_count, HEAD)  56.3 us
    psum x1, waiting for transfers between devices, per_device(): lax.psum(jnp.dot(attended_low, w_out, preferred_element_type=jnp.float32)...  52.6 us
    psum x1, waiting for transfers between devices, per_device(): lax.psum(jnp.dot(d_proj, wb_qkv.T, preferred_element_type=jnp.float32).as...  42.6 us
  transfers between devices with their start and end apart: 12, of which 11 were waited for; matrix products, arithmetic and copies ran while one was open for 19% of the time, Pallas kernels for 0%

commit v1 on v0

--- a/solution.py
+++ b/solution.py
@@ -183,8 +183,33 @@
         .astype(jnp.bfloat16)
         .reshape(slot_count, ctx_tokens, head_cols)
     )
+
+    def _find_circles(work_x):
+        upper, local_now, big = (
+            jax.lax.axis_size("ctx"),
+            jax.lax.axis_index("ctx"),
+            work_x.shape[1],
+        )
+        arrivals = list(map(lambda dd: (dd, (dd + 1) % upper), range(upper)))
+        pile = list(map(lambda dd: (dd, (dd - 1) % upper), range(upper)))
+        piece_now = jnp.zeros((*work_x.shape[:1], upper * big, *work_x.shape[2:]), work_x.dtype)
+        piece_now = lax.dynamic_update_slice_in_dim(piece_now, work_x, local_now * big, axis=1)
+        carry_out = seen_now = work_x
+        field_out = upper // 2
+        for hop_no in [*range(1, field_out + 1)]:
+            carry_out = jax.lax.ppermute(carry_out, "ctx", arrivals)
+            piece_now = lax.dynamic_update_slice_in_dim(
+                piece_now, carry_out, (local_now - hop_no) % upper * big, axis=1
+            )
+            if hop_no < upper - field_out:
+                seen_now = jax.lax.ppermute(seen_now, "ctx", pile)
+                piece_now = lax.dynamic_update_slice_in_dim(
+                    piece_now, seen_now, (local_now + hop_no) % upper * big, axis=1
+                )
+        return piece_now
+
     keys_all, values_all = (
-        lax.all_gather(key_rows, "ctx", axis=1, tiled=True),
+        _find_circles(key_rows),
         lax.all_gather(value_rows, "ctx", axis=1, tiled=True),
     )
     query_slots = queries.reshape(slot_count, ctx_tokens, head_cols)

time: 1030 us -> 1060 us (1.029)
  local copies, waits for them, and re-layouts: 215 us -> 231 us
  starting transfers between devices: 2.24 us -> 16.5 us
  waiting for transfers between devices: 597 us -> 585 us
    all_gather x1 -> x0, waiting for transfers between devices: 27.4 us -> none  [per_device(): lax.all_gather(key_rows, 'ctx', axis=1, tiled=True)]
    ppermute x0 -> x3, waiting for transfers between devices: none -> 22.9 us  [the longest x2 21.2 us: _find_circles(): carry_out = jax.lax.ppermute(carry_out, 'ctx', arrivals)]
    ppermute x0 -> x3, starting transfers between devices: none -> 14.5 us  [the longest x2 11.5 us: _find_circles(): carry_out = jax.lax.ppermute(carry_out, 'ctx', arrivals)]
    unnamed x164 -> x162, local copies, waits for them, and re-layouts: 19.5 us -> 23 us
    unnamed x14 -> x13, waiting for transfers between devices: 85.7 us -> 85.9 us
  transfers between devices with their start and end apart: 12 -> 14, of which waited for: 11 -> 12; matrix products, arithmetic and copies ran while one was open for 19% -> 21% of each run, Pallas kernels for 0% -> 0%
where the time goes in v1:
time: 1060 us; the launch traced here: 1050 us
  waiting for transfers between devices  585 us (55%)
  local copies, waits for them, and re-layouts  231 us (22%)
  other arithmetic  108 us (10%)
  matrix products  72.9 us (7%)
  blocking collectives  19.3 us (2%)
  starting transfers between devices  16.5 us (2%)
  between operations  15.7 us (1%)
    reduce_scatter x1, waiting for transfers between devices, per_device(): lax.psum_scatter(blocks_grad, ('shard', 'ctx'), scatter_dimension=0, tile...  162 us
    unnamed x13, waiting for transfers between devices  85.9 us
    all_gather x1, waiting for transfers between devices, per_device(): lax.all_gather(master_blocks.astype(jnp.bfloat16), ('shard', 'ctx'), axis...  78.2 us
    psum x1, waiting for transfers between devices, per_device(): lax.psum(jnp.dot(d_gate_low, wb_up.T, preferred_element_type=jnp.float32)...  67.9 us
    psum x1, waiting for transfers between devices, per_device(): lax.psum(jnp.dot(act_low, w_down, preferred_element_type=jnp.float32), 'tp')  67.8 us
    reshape x4, local copies, waits for them, and re-layouts, pick_blocks(): picked.reshape(clipped.shape[0], clipped.shape[1] * BLOCK, head_count, HEAD)  56.3 us
    psum x1, waiting for transfers between devices, per_device(): lax.psum(jnp.dot(attended_low, w_out, preferred_element_type=jnp.float32)...  54.7 us
    psum x1, waiting for transfers between devices, per_device(): lax.psum(jnp.dot(d_proj, wb_qkv.T, preferred_element_type=jnp.float32).as...  42.4 us
  transfers between devices with their start and end apart: 14, of which 12 were waited for; matrix products, arithmetic and copies ran while one was open for 21% of the time, Pallas kernels for 0%

profile of v1, /device:TPU:0, one launch (start us, length us, event | category | flops | bytes accessed | tf_op | source)
XLA Modules:
  0.0 1048.5 jit_solution(9021119619010124140)
XLA Ops:
  14.6 78.2 %all-gather.4.cloned.1.call-done = bf16[192,96,96]{2,1,0:T(8,128)(2,1)} async-done(((bf16[24,96,96]{2,1,0:T(8,128)(2,1)}), bf16[192,96,96]{2,1,0:T(8,128)(2,1)}) %all-gather.4.cloned.1.call-update) | async-done | bytes 3538960 | tf_op jit(solution)/shard_map/all_gather | solution.py:165
  95.8 2.8 fusion.29
  104.1 3.0 collective-permute-start.1
  108.2 14.2 %collective-permute-done = bf16[1,1024,192]{1,2,0:T(8,128)(2,1)} collective-permute-done((bf16[1,1024,192]{1,2,0:T(8,128)(2,1)}, bf16[1,1024,192]{1,2,0:T(8,128)(2,1)}, u32[]{:S(2)}, u32[]{:S(2)}) %collective-permute-start) | collective-permute-done | bytes 393248 | tf_op jit(solution)/shard_map/ppermute | solution.py:200
  122.4 10.6 %collective-permute-start.2 = (bf16[1,1024,192]{1,2,0:T(8,128)(2,1)}, bf16[1,1024,192]{1,2,0:T(8,128)(2,1)}, u32[]{:S(2)}, u32[]{:S(2)}) collective-permute-start(bf16[1,1024,192]{1,2,0:T(8,128)(2,1)} %collective-permute-done), channel_id=1, source_target_pairs={{0,4},{4,8},{8,12},{12,0},{1,5},{5,9},{9,13},{13,1},{2,6},{6,10},{... | collective-permute-start | bytes 1179656 | tf_op jit(solution)/shard_map/ppermute | solution.py:200
  146.6 7.0 collective-permute-done.2
  159.4 15.9 %reshape.557 = bf16[16,512,3,64]{3,2,1,0:T(4,128)(2,1)} reshape(bf16[128,64,192]{2,1,0:T(8,128)(2,1)} %gather_fusion.1) | data formatting | bytes 6291456 | tf_op jit(solution)/shard_map/reshape | solution.py:73
  175.3 12.3 %copy.115 = bf16[16,512,3,64]{1,3,2,0:T(8,128)(2,1)} copy(bf16[16,512,3,64]{3,2,1,0:T(4,128)(2,1)} %reshape.557) | data formatting | bytes 6291456 | tf_op jit(solution)/shard_map/reshape | solution.py:73
  187.6 3.2 fusion.24
  193.6 3.6 select_reduce_fusion
  197.2 3.2 copy.104
  203.1 15.9 %reshape.556 = bf16[16,512,3,64]{3,2,1,0:T(4,128)(2,1)} reshape(bf16[128,64,192]{2,1,0:T(8,128)(2,1)} %gather_fusion) | data formatting | bytes 6291456 | tf_op jit(solution)/shard_map/reshape | solution.py:73
  219.0 12.2 %copy.116 = bf16[16,512,3,64]{1,3,2,0:T(8,128)(2,1)} copy(bf16[16,512,3,64]{3,2,1,0:T(4,128)(2,1)} %reshape.556) | data formatting | bytes 6291456 | tf_op jit(solution)/shard_map/reshape | solution.py:73
  231.3 6.0 fusion.39
  246.0 3.8 reshape.488
  251.6 3.9 reshape.490
  255.5 54.7 %all-reduce.7.cloned.1.call-done = f32[1024,768]{1,0:T(8,128)} async-done(((f32[1024,768]{1,0:T(8,128)}), f32[1024,768]{1,0:T(8,128)}) %all-reduce.7.cloned.1.call-update) | async-done | bytes 3145744 | tf_op jit(solution)/shard_map/psum | solution.py:250
  318.0 3.8 fusion.62
  322.7 67.8 %all-reduce.9.cloned.1.call-done = f32[1024,768]{1,0:T(8,128)} async-done(((f32[1024,768]{1,0:T(8,128)}), f32[1024,768]{1,0:T(8,128)}) %all-reduce.9.cloned.1.call-update) | async-done | bytes 3145744 | tf_op jit(solution)/shard_map/psum | solution.py:259
  390.5 3.9 fusion.66
  404.5 4.3 convert_reduce_fusion
  410.0 3.1 fusion.72
  413.9 67.9 %all-reduce.11.cloned.1.call-done = f32[1024,768]{1,0:T(8,128)} async-done(((f32[1024,768]{1,0:T(8,128)}), f32[1024,768]{1,0:T(8,128)}) %all-reduce.11.cloned.1.call-update) | async-done | bytes 3145744 | tf_op jit(solution)/shard_map/psum | solution.py:282
  481.9 5.4 multiply_reduce_fusion.1
  493.8 7.2 fusion.20
  501.0 15.0 %copy.145 = f32[16,512,3,64]{3,2,1,0:T(4,128)} copy(f32[16,512,3,64]{1,3,2,0:T(8,128)} %fusion.20) | data formatting | bytes 12582912 | tf_op jit(solution)/shard_map/reshape | solution.py:132
  516.0 18.9 %reshape.551 = f32[128,64,192]{2,1,0:T(8,128)} reshape(f32[16,512,3,64]{3,2,1,0:T(4,128)} %copy.145) | data formatting | bytes 12582912 | tf_op jit(solution)/shard_map/reshape | solution.py:132
  537.4 26.5 %scatter_fusion.1 = f32[64,64,192]{2,1,0:T(8,128)} fusion(f32[64,64,192]{2,1,0:T(8,128)} %broadcast.361.clone, s32[128]{0:T(128)S(1)} %reshape.508, f32[128,64,192]{2,1,0:T(8,128)} %reshape.551), kind=kCustom, calls=%fused_computation.3 | custom fusion | flops 1572864 | bytes 18874880 | tf_op jit(solution)/shard_map/scatter-add | solution.py:132
  569.3 6.7 multiply_reduce_fusion
  576.0 3.9 multiply_convert_fusion
  581.7 3.6 multiply_bitcast_fusion
  585.3 15.1 %copy.144 = f32[16,512,3,64]{3,2,1,0:T(4,128)} copy(f32[16,512,3,64]{1,3,2,0:T(8,128)} %multiply_bitcast_fusion) | data formatting | bytes 12582912 | tf_op jit(solution)/shard_map/reshape | solution.py:127
  600.4 18.9 %reshape.550 = f32[128,64,192]{2,1,0:T(8,128)} reshape(f32[16,512,3,64]{3,2,1,0:T(4,128)} %copy.144) | data formatting | bytes 12582912 | tf_op jit(solution)/shard_map/reshape | solution.py:127
  621.7 26.5 %scatter_fusion = f32[64,64,192]{2,1,0:T(8,128)} fusion(f32[64,64,192]{2,1,0:T(8,128)} %broadcast.361.clone.1, s32[128]{0:T(128)S(1)} %reshape.508, f32[128,64,192]{2,1,0:T(8,128)} %reshape.550), kind=kCustom, calls=%fused_computation.2 | custom fusion | flops 1572864 | bytes 18874880 | tf_op jit(solution)/shard_map/scatter-add | solution.py:127
  653.8 4.3 fusion.61
  660.7 4.3 copy.136
  669.0 4.4 copy.135
  685.9 3.0 reduce-scatter.10.cloned.1.call-done
  688.9 4.1 convolution_convert_fusion
  702.2 7.8 pad_maximum_fusion
  710.6 19.3 %pmax.7 = f32[3]{0:T(128)S(1)} all-reduce(f32[3]{0:T(128)S(1)} %broadcast_maximum_fusion), channel_id=1, replica_groups=mesh['shard'=2,'ctx'=4,'tp'=4] {'shard','ctx'}, use_global_device_ids=true, to_apply=%region_32.33 | all-reduce | flops 3 | bytes 24 | tf_op jit(solution)/shard_map/pmax | solution.py:264
  730.9 22.4 %reduce-scatter.16.cloned.1.call-done = f32[96,6]{1,0:T(8,128)} async-done(((f32[768,6]{1,0:T(8,128)}), f32[96,6]{1,0:T(8,128)}) %reduce-scatter.16.cloned.1.call-update) | async-done | bytes 2320
  755.6 63.3 %reduce-scatter.18.cloned.1.call-done = f32[144,1]{1,0:T(8,128)} async-done(((f32[1152,1]{1,0:T(8,128)}), f32[144,1]{1,0:T(8,128)}) %reduce-scatter.18.cloned.1.call-update) | async-done | bytes 592
  821.2 42.4 %all-reduce.13.cloned.1.call-done = bf16[1024,768]{1,0:T(8,128)(2,1)} async-done(((bf16[1024,768]{1,0:T(8,128)(2,1)}), bf16[1024,768]{1,0:T(8,128)(2,1)}) %all-reduce.13.cloned.1.call-update) | async-done | bytes 1572880 | tf_op jit(solution)/shard_map/psum | solution.py:327
  863.6 3.9 fusion.26
  867.5 162.4 %reduce-scatter.14.cloned.1.call-done = f32[24,96,96]{2,1,0:T(8,128)} async-done(((f32[192,96,96]{2,1,0:T(8,128)}), f32[24,96,96]{2,1,0:T(8,128)}) %reduce-scatter.14.cloned.1.call-update) | async-done | bytes 884752 | tf_op jit(solution)/shard_map/reduce_scatter | solution.py:337
  1034.9 3.2 fusion.36
  1038.1 3.6 fusion.37
  (310 shorter events, 135.4 us)
Async XLA Ops:
  7.2 1022.8 %copy-start = (f32[24,96,96]{2,1,0:T(8,128)S(1)}, f32[24,96,96]{2,1,0:T(8,128)}, u32[]{:S(2)}) copy-start(f32[24,96,96]{2,1,0:T(8,128)} %param.21) | copy-start | bytes 2654212
  7.2 85.6 %all-gather.4.cloned.1.call-start = ((), (), s32[]{:S(2)}) async-start(), calls=%async_computation.5 | async-start | bytes 5308416 | tf_op jit(solution)/shard_map/all_gather | solution.py:165
  9.5 187.7 %all-gather.6.cloned.1.call-start = ((), (), s32[]{:S(2)}) async-start(), calls=%async_computation.13 | async-start | bytes 1966080 | tf_op jit(solution)/shard_map/all_gather | solution.py:213
  98.7 5.2 copy-start.71
  100.1 36.2 %slice-start.1 = ((bf16[192,96,96]{2,1,0:T(8,128)(2,1)}), bf16[16,96,96]{2,1,0:T(8,128)(2,1)S(1)}, s32[]{:S(2)}) async-start(bf16[192,96,96]{2,1,0:T(8,128)(2,1)} %all-gather.4.cloned.1.call-done), calls=%async_computation.17 | async-start | bytes 786432 | tf_op jit(solution)/shard_map/slice | solution.py:49
  101.0 209.2 %all-reduce.7.cloned.1.call-start = ((), (), s32[]{:S(2)}) async-start(), calls=%async_computation.6 | async-start | bytes 6291456 | tf_op jit(solution)/shard_map/psum | solution.py:250
  103.0 19.4 %collective-permute-start = (bf16[1,1024,192]{1,2,0:T(8,128)(2,1)}, bf16[1,1024,192]{1,2,0:T(8,128)(2,1)}, u32[]{:S(2)}, u32[]{:S(2)}) collective-permute-start(bf16[1,1024,192]{1,2,0:T(8,128)(2,1)} %fusion.48), channel_id=1, source_target_pairs={{0,4},{4,8},{8,12},{12,0},{1,5},{5,9},{9,13},{13,1},{2,6},{6,10},{... | collective-permute-start | bytes 1179656 | tf_op jit(solution)/shard_map/ppermute | solution.py:200
  104.1 38.3 %collective-permute-start.1 = (bf16[1,1024,192]{1,2,0:T(8,128)(2,1)}, bf16[1,1024,192]{1,2,0:T(8,128)(2,1)}, u32[]{:S(2)}, u32[]{:S(2)}) collective-permute-start(bf16[1,1024,192]{1,2,0:T(8,128)(2,1)} %fusion.48), channel_id=1, source_target_pairs={{0,12},{4,0},{8,4},{12,8},{1,13},{5,1},{9,5},{13,9},{2,14},{6,2},{... | collective-permute-start | bytes 1179656 | tf_op jit(solution)/shard_map/ppermute | solution.py:205
  122.4 31.2 %collective-permute-start.2 = (bf16[1,1024,192]{1,2,0:T(8,128)(2,1)}, bf16[1,1024,192]{1,2,0:T(8,128)(2,1)}, u32[]{:S(2)}, u32[]{:S(2)}) collective-permute-start(bf16[1,1024,192]{1,2,0:T(8,128)(2,1)} %collective-permute-done), channel_id=1, source_target_pairs={{0,4},{4,8},{8,12},{12,0},{1,5},{5,9},{9,13},{13,1},{2,6},{6,10},{... | collective-permute-start | bytes 1179656 | tf_op jit(solution)/shard_map/ppermute | solution.py:200
  175.3 12.3 %copy-start.11 = (bf16[16,64,3,64]{1,0,3,2:T(8,128)(2,1)S(1)}, bf16[16,64,3,64]{1,0,3,2:T(8,128)(2,1)}, u32[]{:S(2)}) copy-start(bf16[16,64,3,64]{1,0,3,2:T(8,128)(2,1)} %reshape_squeeze_reshape.7) | copy-start | bytes 1179652
  187.6 6.0 copy-start.20
  190.9 40.4 %copy-start.36 = (f32[16,3,64]{2,1,0:T(4,128)}, f32[16,3,64]{2,1,0:T(4,128)S(1)}, u32[]{:S(2)}) copy-start(f32[16,3,64]{2,1,0:T(4,128)S(1)} %get-tuple-element.47) | copy-start | bytes 36868
  197.2 34.1 %copy-start.38 = (f32[16,3,64]{2,1,0:T(4,128)}, f32[16,3,64]{2,1,0:T(4,128)S(1)}, u32[]{:S(2)}) copy-start(f32[16,3,64]{2,1,0:T(4,128)S(1)} %get-tuple-element.14) | copy-start | bytes 36868
  231.2 7.0 copy-start.31
  240.6 149.9 %all-reduce.9.cloned.1.call-start = ((), (), s32[]{:S(2)}) async-start(), calls=%async_computation.7 | async-start | bytes 6291456 | tf_op jit(solution)/shard_map/psum | solution.py:259
  242.1 71.0 %copy-start.42 = (f32[768]{0:T(1024)}, f32[768]{0:T(1024)S(1)}, u32[]{:S(2)}) copy-start(f32[768]{0:T(1024)S(1)} %get-tuple-element.22) | copy-start | bytes 9220
  242.1 71.0 %copy-start.48 = (f32[768]{0:T(1024)}, f32[768]{0:T(1024)S(1)}, u32[]{:S(2)}) copy-start(f32[768]{0:T(1024)S(1)} %get-tuple-element.21) | copy-start | bytes 9220
  251.6 58.6 %copy-start.22 = (bf16[1,1024,768]{2,1,0:T(8,128)(2,1)S(1)}, bf16[1,1024,768]{2,1,0:T(8,128)(2,1)}, u32[]{:S(2)}) copy-start(bf16[1,1024,768]{2,1,0:T(8,128)(2,1)} %param.12) | copy-start | bytes 4718596
  321.8 160.0 %all-reduce.11.cloned.1.call-start = ((), (), s32[]{:S(2)}) async-start(), calls=%async_computation.8 | async-start | bytes 6291456 | tf_op jit(solution)/shard_map/psum | solution.py:282
  400.9 7.9 copy-start.5
  400.9 7.9 copy-start.44
  401.8 7.0 copy-start.25
  413.1 68.7 %copy-start.41 = (f32[1024]{0:T(1024)S(1)}, f32[1024]{0:T(1024)}, u32[]{:S(2)}) copy-start(f32[1024]{0:T(1024)} %copy-done.40) | copy-start | bytes 12292
  413.1 68.7 %copy-start.43 = (f32[768]{0:T(1024)S(1)}, f32[768]{0:T(1024)}, u32[]{:S(2)}) copy-start(f32[768]{0:T(1024)} %copy-done.42) | copy-start | bytes 9220
  413.1 68.7 %copy-start.45 = (f32[1024]{0:T(1024)S(1)}, f32[1024]{0:T(1024)}, u32[]{:S(2)}) copy-start(f32[1024]{0:T(1024)} %copy-done.44) | copy-start | bytes 12292
  413.2 270.4 %reduce-scatter.12.cloned.1.call-start = ((), (), s32[]{:S(2)}) async-start(), calls=%async_computation.10 | async-start | bytes 1966080 | tf_op jit(solution)/shard_map/reduce_scatter | solution.py:316
  413.9 73.3 %copy-start.50 = (f32[1024]{0:T(1024)S(1)}, f32[1024]{0:T(1024)}, u32[]{:S(2)}) copy-start(f32[1024]{0:T(1024)} %copy-done.49) | copy-start | bytes 12292
  481.9 5.4 copy-start.3
  493.7 7.3 copy-start.10
  569.1 119.8 %reduce-scatter.10.cloned.1.call-start = ((), (), s32[]{:S(2)}) async-start(), calls=%async_computation.9 | async-start | bytes 1966080 | tf_op jit(solution)/shard_map/reduce_scatter | solution.py:313
  576.0 5.6 copy-start.12
  653.5 99.8 %reduce-scatter.16.cloned.1.call-start = ((), (), s32[]{:S(2)}) async-start(), calls=%async_computation.14 | async-start | bytes 442368
  666.4 7.0 copy-start.55
  669.0 5.0 copy-start.59
  669.0 5.6 copy-start.58
  669.0 6.1 copy-start.8
  669.0 6.1 copy-start.9
  677.0 5.4 copy-start.56
  677.0 5.4 copy-start.53
  677.0 5.4 copy-start.52
  680.7 8.2 copy-start.35
  683.5 135.4 %reduce-scatter.18.cloned.1.call-start = ((), (), s32[]{:S(2)}) async-start(), calls=%async_computation.15 | async-start | bytes 663552
  685.8 177.8 %all-reduce.13.cloned.1.call-start = ((), (), s32[]{:S(2)}) async-start(), calls=%async_computation.11 | async-start | bytes 3145728 | tf_op jit(solution)/shard_map/psum | solution.py:327
  693.1 336.9 %reduce-scatter.14.cloned.1.call-start = ((), (), s32[]{:S(2)}) async-start(), calls=%async_computation.12 | async-start | bytes 10616832 | tf_op jit(solution)/shard_map/reduce_scatter | solution.py:337
  754.2 109.4 %copy-start.57 = (f32[6,96]{1,0:T(8,128)}, f32[6,96]{1,0:T(8,128)S(1)}, u32[]{:S(2)}) copy-start(f32[6,96]{1,0:T(8,128)S(1)} %copy.147) | copy-start | bytes 6916
  819.8 43.8 %copy-start.64 = (f32[1,144]{1,0:T(1,128)}, f32[1,144]{1,0:T(1,128)S(1)}, u32[]{:S(2)}) copy-start(f32[1,144]{1,0:T(1,128)S(1)} %copy.149) | copy-start | bytes 1732
  867.5 164.9 %copy-start.17 = (f32[24,96,96]{2,1,0:T(8,128)S(1)}, f32[24,96,96]{2,1,0:T(8,128)}, u32[]{:S(2)}) copy-start(f32[24,96,96]{2,1,0:T(8,128)} %param.16) | copy-start | bytes 2654212
  867.5 164.9 %copy-start.26 = (f32[24,96,96]{2,1,0:T(8,128)S(1)}, f32[24,96,96]{2,1,0:T(8,128)}, u32[]{:S(2)}) copy-start(f32[24,96,96]{2,1,0:T(8,128)} %param.22) | copy-start | bytes 2654212
  (46 other events, 103.7 us)
Sparse Core Ops, SparseCore 0:
  10.7 82.0 all-gather.3
  101.1 55.7 all-gather.5
  240.7 69.4 all-reduce.6
  322.0 68.5 all-reduce.8
  413.3 68.5 all-reduce.10
  569.2 35.3 reduce-scatter.11
  653.7 35.1 reduce-scatter.9
  692.2 61.0 reduce-scatter.15
  757.2 61.6 reduce-scatter.17
  821.7 41.8 all-reduce.12
  867.7 162.1 reduce-scatter.13
